TPU v7x, 128 devices: a whole 4x4x4 slice. The times are simulated.
128 devices in a mesh: row: 8 (over y, core), col: 16 (over z, x).
Axes of the slice: x: 4, y: 4, z: 4, core: 2. Of those that a mesh axis runs over, the one named last changes fastest.
Arguments:
- amplitudes: float32 [96, 256, 1024], P('col', None, 'row'), may hold values from -6 to 6
- interaction: float32 [16384, 16384], P('row', 'col'), may hold values from -0.5 to 0.5, as said below
- tile_counts: int32 [16], replicated, may hold values from 2 to 6, as said below
- tile_block: int32 [96], replicated, may hold values from -1 to 63, as said below
- recouple_sign: int32 [96], replicated, may hold values from 0 to 1
- orbit_perm: int32 [96, 256], replicated, may hold values from 0 to 255, each once within a row
- particle_energy: float32 [96, 256], P('col'), may hold values from -2 to 2
Outputs:
- sigma: float32 [96, 256, 1024], P('col', None, 'row')
Inputs may be any that keep to these rules, and one draw needn't show every extreme that they name: Owner c holds its live tiles in its first tile_counts[c] slots; the counts sum to 64, and some owner holds 6. `tile_block`: live slots map one to one onto the 64 cross-channel tiles, and slots that are not live hold -1; two live tiles of one owner never lie in the same aligned group of 4 cross-channel tiles. interaction equals its transpose.
All inputs are finite; a program needn't handle non-finite values.
Results may differ from a plain program's by a relative error of at most 0.000061.
Values sent between devices are 32-bit elements; how exact they have to be, the bound alone decides.
A program may use at most 128 MiB of HBM per device.

v0:
```python
import jax
import jax.numpy as jnp
from jax import lax
from jax.sharding import PartitionSpec as P


def split_up(value, dim, length):
    before, after = (value.shape[:dim], value.shape[dim + 1 :])
    return jnp.moveaxis(value.reshape(*before, length, -1, *after), dim, 0)


def sum_at_owner(value, axis, dim):
    length = lax.axis_size(axis)
    tiles = lax.all_to_all(split_up(value, dim, length), axis, 0, 0, tiled=True)
    return jnp.sum(tiles, axis=0)


def tile_recouple(tiles, phases, orders):
    moved = jax.vmap(lambda single, ordering: jnp.take(single, ordering, axis=0))(tiles, orders)
    return moved * phases[:, None, None]


def local(
    amplitudes, interaction, tile_counts, tile_block, recouple_sign, orbit_perm, particle_energy
):
    column_index = lax.axis_index("col")
    row_index = lax.axis_index("row")
    column_count = lax.axis_size("col")
    slots, tile_rows, narrow_cols = amplitudes.shape
    row_blocks = interaction.shape[0] // tile_rows
    col_blocks = interaction.shape[1] // tile_rows
    tile_total = tile_block.shape[0]
    slot_ids = jnp.arange(slots, dtype=jnp.int32)
    is_live = slot_ids < jnp.take(tile_counts, column_index)
    live_mask = is_live.astype(jnp.float32)[:, None, None]
    own_block = jnp.where(
        is_live, lax.dynamic_slice_in_dim(tile_block, column_index * slots, slots), -1
    )
    all_phases = (1 - 2 * recouple_sign).astype(jnp.float32)
    own_phases = lax.dynamic_slice_in_dim(all_phases, column_index * slots, slots)
    own_orders = lax.dynamic_slice_in_dim(orbit_perm, column_index * slots, slots, 0)
    diagonal = particle_energy[:, :, None] * amplitudes
    tile_ids = jnp.arange(tile_total, dtype=jnp.int32)
    peer_ids = jnp.arange(column_count, dtype=jnp.int32)

    def tiles_of(blocks):
        matches = tile_block[None, :] == blocks[:, None]
        return jnp.sum(jnp.where(matches, tile_ids[None, :], 0), axis=1)

    target_col = own_block // col_blocks
    my_blocks = column_index * col_blocks + jnp.arange(col_blocks, dtype=jnp.int32)
    block_tiles = tiles_of(my_blocks)
    widened = lax.all_gather(amplitudes, "row", axis=2, tiled=True)
    widened = tile_recouple(widened, own_phases, own_orders)
    group_blocks = row_index * row_blocks + jnp.arange(row_blocks, dtype=jnp.int32)
    group_tiles = tiles_of(group_blocks)
    is_owned = group_tiles // slots == column_index
    placed = (
        jnp.take(widened, group_tiles % slots, axis=0) * is_owned.astype(jnp.float32)[:, None, None]
    )
    crossed = lax.psum(placed.reshape(row_blocks * tile_rows, widened.shape[2]), "col")
    partial_cols = lax.dot_general(
        interaction,
        crossed,
        (((0,), (0,)), ((), ())),
        precision=lax.Precision.HIGHEST,
        preferred_element_type=jnp.float32,
    )
    own_part = sum_at_owner(partial_cols, "row", 1)
    blocks_here = own_part.reshape(col_blocks, tile_rows, narrow_cols)
    block_inverse = jnp.argsort(jnp.take(orbit_perm, block_tiles, axis=0), axis=1)
    blocks_here = tile_recouple(blocks_here, jnp.take(all_phases, block_tiles), block_inverse)
    block_owner = block_tiles // slots
    choose_mask = block_owner[None, :] == peer_ids[:, None]
    choose_block = jnp.sum(
        jnp.where(choose_mask, jnp.arange(col_blocks, dtype=jnp.int32)[None, :], 0), axis=1
    )
    choose_weight = jnp.max(choose_mask.astype(jnp.float32), axis=1)
    outgoing = jnp.take(blocks_here, choose_block, axis=0) * choose_weight[:, None, None]
    arrived = lax.all_to_all(outgoing, "col", split_axis=0, concat_axis=0, tiled=True)
    returned = jnp.take(arrived, jnp.clip(target_col, 0, column_count - 1), axis=0)
    return (returned + diagonal) * live_mask


def solution(mesh):
    placed = (P("col", None, "row"), P("row", "col"), P(), P(), P(), P(), P("col", None))
    return jax.shard_map(
        local, mesh=mesh, in_specs=placed, out_specs=P("col", None, "row"), check_vma=False
    )
```

profile of v0, /device:TPU:0, one launch (start us, length us, event | category | flops | bytes accessed | tf_op | source)
XLA Modules:
  0.0 393.0 jit_solution(7255663869322990882)
XLA Ops:
  7.4 0.7 all-gather.2.cloned.1.call-update
  8.1 0.0 all-reduce.2.cloned.1.call-start
  8.1 0.7 subtract_convert_fusion
  8.8 0.1 dynamic_slice.11
  8.9 0.7 bitcast_or_fusion
  9.6 0.8 select_reduce_fusion
  10.5 0.1 broadcast_bitcast_fusion
  10.6 0.1 broadcast_in_dim.144
  10.7 0.7 compare_and_fusion
  11.4 45.4 %all-gather.2.cloned.1.call-done = f32[6,256,1024]{2,1,0:T(8,128)} async-done(((f32[6,256,128]{2,1,0:T(8,128)}), f32[6,256,1024]{2,1,0:T(8,128)}) %all-gather.2.cloned.1.call-update) | async-done | bytes 6291472 | tf_op jit(solution)/shard_map/all_gather | solution.py:53
  56.8 30.5 %gather_fusion.5 = f32[1536,1024]{1,0:T(8,128)} fusion(f32[6,256,1024]{2,1,0:T(8,128)} %all-gather.2.cloned.1.call-done, s32[1536]{0:T(1024)S(1)} %reshape.221), kind=kCustom, calls=%fused_computation.5 | custom fusion | bytes 12595200 | tf_op jit(solution)/shard_map/vmap(jit(_take))/gather | solution.py:19
  87.3 4.9 %select_multiply_fusion = f32[6,256,1024]{2,1,0:T(8,128)} fusion(f32[6,256,1024]{2,1,0:T(8,128)} %bitcast.45, f32[6]{0:T(128)S(1)} %dynamic_slice.11, pred[6,256]{1,0:T(8,128)(4,1)S(1)} %compare_and_fusion), kind=kLoop, calls=%fused_computation.9 | loop fusion | flops 3145728 | bytes 12584472 | tf_op jit(solution)/shard_map/mul | solution.py:20
  92.2 7.1 %gather_fusion.1 = f32[8,256,1024]{2,1,0:T(8,128)} fusion(f32[6,256,1024]{2,1,0:T(8,128)} %select_multiply_fusion, s32[1024]{0:T(1024)S(1)} %pad_clamp_fusion.2), kind=kCustom, calls=%fused_computation.1 | custom fusion | bytes 16777248 | tf_op jit(solution)/shard_map/jit(_take)/gather | solution.py:59
  99.3 5.8 %fusion = f32[2048,1024]{1,0:T(8,128)} fusion(f32[8,256,1024]{2,1,0:T(8,128)} %gather_fusion.1, f32[2048]{0:T(1024)S(1)} %bitcast.48, pred[2048]{0:T(1024)(128)(4,1)S(1)} %broadcast_in_dim.145), kind=kLoop, calls=%fused_computation.8 | loop fusion | flops 4194304 | bytes 16787456 | tf_op jit(solution)/shard_map/mul | solution.py:59
  105.1 0.0 all-reduce.2.cloned.1.call-update
  105.1 142.9 %all-reduce.2.cloned.1.call-done = f32[2048,1024]{1,0:T(8,128)} async-done(((f32[2048,1024]{1,0:T(8,128)}), f32[2048,1024]{1,0:T(8,128)}) %all-reduce.2.cloned.1.call-update) | async-done | bytes 8388624 | tf_op jit(solution)/shard_map/psum | solution.py:61
  248.1 31.6 %fusion.5 = f32[1024,1024]{1,0:T(8,128)} fusion(f32[2048,1024]{1,0:T(8,128)} %all-reduce.2.cloned.1.call-done, f32[2048,1024]{1,0:T(8,128)} %param.8), kind=kOutput, calls=%fused_computation.61 | convolution fusion | flops 25769803776 | bytes 20971520 | tf_op jit(solution)/shard_map/dot_general | solution.py:62
  279.7 4.7 %all-to-all-start = ((f32[8,1024,128]{1,2,0:T(8,128)}), f32[8,1024,128]{1,2,0:T(8,128)}, u32[]{:S(2)}, u32[]{:S(2)}) async-start(f32[8,1024,128]{1,2,0:T(8,128)} %bitcast.46), calls=%async_computation | async-start | bytes 8388608 | tf_op jit(solution)/shard_map/all_to_all | solution.py:14
  284.4 0.2 sort.19.cloned.1.call-start
  284.6 0.2 select_reduce_fusion.2
  284.8 0.6 gather_fusion.2
  285.5 1.5 gather_fusion
  286.9 0.7 broadcast_select_fusion
  287.6 0.6 iota.37
  288.2 0.0 sort.19.cloned.1.call-update
  288.2 0.1 select_reduce_fusion.1
  288.3 0.1 convert_reduce_fusion
  288.4 2.7 sort.19.cloned.1.call-done
  291.1 0.7 fusion.1
  291.8 0.7 compare_and_fusion.1
  292.5 41.5 %all-to-all-done = f32[8,1024,128]{1,2,0:T(8,128)} async-done(((f32[8,1024,128]{1,2,0:T(8,128)}), f32[8,1024,128]{1,2,0:T(8,128)}, u32[]{:S(2)}, u32[]{:S(2)}) %all-to-all-start) | async-done | bytes 4194336 | tf_op jit(solution)/shard_map/all_to_all | solution.py:14
  334.0 2.6 reduce_sum.44
  336.6 0.2 copy.9
  336.8 6.8 %gather_fusion.6 = f32[1024,128]{1,0:T(8,128)S(1)} fusion(f32[4,256,128]{2,1,0:T(8,128)S(1)} %bitcast.44, s32[1024]{0:T(1024)S(1)} %bitcast.43), kind=kCustom, calls=%fused_computation.6 | custom fusion | bytes 1056768 | tf_op jit(solution)/shard_map/vmap(jit(_take))/gather | solution.py:19
  343.6 0.2 select_multiply_fusion.2
  343.8 0.0 copy-start.3
  343.9 0.0 copy-start
  343.9 0.0 copy-start.1
  343.9 0.7 gather_fusion.3
  344.6 1.6 select_multiply_fusion.1
  346.2 4.5 %all-to-all-start.1 = ((f32[16,256,128]{2,1,0:T(8,128)}), f32[16,256,128]{2,1,0:T(8,128)S(1)}, u32[]{:S(2)}, u32[]{:S(2)}) async-start(f32[16,256,128]{2,1,0:T(8,128)} %select_multiply_fusion.1), calls=%async_computation.1 | async-start | bytes 4194304 | tf_op jit(solution)/shard_map/all_to_all | solution.py:80
  350.8 0.0 copy-done.3
  350.8 0.6 dynamic-slice.2
  352.0 0.1 compare_and_fusion.5
  352.1 29.7 %all-to-all-done.1 = f32[16,256,128]{2,1,0:T(8,128)S(1)} async-done(((f32[16,256,128]{2,1,0:T(8,128)}), f32[16,256,128]{2,1,0:T(8,128)S(1)}, u32[]{:S(2)}, u32[]{:S(2)}) %all-to-all-start.1) | async-done | bytes 2097184 | tf_op jit(solution)/shard_map/all_to_all | solution.py:80
  381.8 1.5 gather_fusion.4
  383.2 0.0 copy-done.1
  383.2 2.3 add_multiply_fusion
  (21 shorter events, 0.1 us)
Async XLA Ops:
  7.4 49.4 %all-gather.2.cloned.1.call-start = ((), (), s32[]{:S(2)}) async-start(), calls=%async_computation.2 | async-start | bytes 7077888 | tf_op jit(solution)/shard_map/all_gather | solution.py:53
  8.1 240.0 %all-reduce.2.cloned.1.call-start = ((), (), s32[]{:S(2)}) async-start(), calls=%async_computation.3 | async-start | bytes 16777216 | tf_op jit(solution)/shard_map/psum | solution.py:61
  279.7 4.9 %copy-start.2 = (s32[96]{0:T(128)S(1)}, s32[96]{0:T(128)}, u32[]{:S(2)}) copy-start(s32[96]{0:T(128)} %param.10) | copy-start | bytes 1156
  279.7 54.3 %all-to-all-start = ((f32[8,1024,128]{1,2,0:T(8,128)}), f32[8,1024,128]{1,2,0:T(8,128)}, u32[]{:S(2)}, u32[]{:S(2)}) async-start(f32[8,1024,128]{1,2,0:T(8,128)} %bitcast.46), calls=%async_computation | async-start | bytes 8388608 | tf_op jit(solution)/shard_map/all_to_all | solution.py:14
  284.4 6.7 %sort.19.cloned.1.call-start = ((), (), s32[]{:S(2)}) async-start(), calls=%async_computation.4 | async-start | bytes 24608 | tf_op jit(solution)/shard_map/jit(argsort)/sort | solution.py:71
  343.8 6.9 %copy-start.3 = (s32[16]{0:T(128)S(1)}, s32[16]{0:T(128)}, u32[]{:S(2)}) copy-start(s32[16]{0:T(128)} %param.9) | copy-start | bytes 196
  343.9 39.4 %copy-start = (f32[6,256,128]{2,1,0:T(8,128)S(1)}, f32[6,256,128]{2,1,0:T(8,128)}, u32[]{:S(2)}) copy-start(f32[6,256,128]{2,1,0:T(8,128)} %param.7) | copy-start | bytes 2359300
  343.9 39.4 %copy-start.1 = (f32[6,256]{1,0:T(8,128)S(1)}, f32[6,256]{1,0:T(8,128)}, u32[]{:S(2)}) copy-start(f32[6,256]{1,0:T(8,128)} %param.13) | copy-start | bytes 18436
  346.2 35.5 %all-to-all-start.1 = ((f32[16,256,128]{2,1,0:T(8,128)}), f32[16,256,128]{2,1,0:T(8,128)S(1)}, u32[]{:S(2)}, u32[]{:S(2)}) async-start(f32[16,256,128]{2,1,0:T(8,128)} %select_multiply_fusion.1), calls=%async_computation.1 | async-start | bytes 4194304 | tf_op jit(solution)/shard_map/all_to_all | solution.py:80
Sparse Core Ops, SparseCore 0:
  9.8 46.9 all-gather.1
  105.3 142.7 all-reduce.1
Sparse Core Ops, SparseCore 1:
  288.3 2.5 sort.21.cloned.1.call-done
  (1 shorter events, 0.0 us)
where the time goes:
time: 394 us; the launch traced here: 393 us
  waiting for transfers between devices  260 us (66%)
  local copies, waits for them, and re-layouts  53.2 us (14%)
  matrix products  31.6 us (8%)
  other arithmetic  23.1 us (6%)
  between operations  15.6 us (4%)
  starting transfers between devices  9.24 us (2%)
    psum x1, waiting for transfers between devices, local(): lax.psum(placed.reshape(row_blocks * tile_rows, widened.shape[2]), 'col')  143 us
    all_gather x1, waiting for transfers between devices, local(): widened = lax.all_gather(amplitudes, 'row', axis=2, tiled=True)  45.4 us
    all_to_all x1, waiting for transfers between devices, sum_at_owner(): tiles = lax.all_to_all(split_up(value, dim, length), axis, 0, 0, tiled=True)  41.5 us
    gather x3, local copies, waits for them, and re-layouts, tile_recouple(): jnp.take(single, ordering, axis=0)  37.3 us
    dot_general x1, matrix products, local(): lax.dot_general(interaction, crossed, (((0,), (0,)), ((), ())), precision...  31.6 us
    all_to_all x1, waiting for transfers between devices, local(): lax.all_to_all(outgoing, 'col', split_axis=0, concat_axis=0, tiled=True)  29.7 us
  transfers between devices with their start and end apart: 4, of which 4 were waited for; matrix products, arithmetic and copies ran while one was open for 2% of the time, Pallas kernels for 0%

commit v1 on v0

--- a/solution.py
+++ b/solution.py
@@ -2,6 +2,12 @@
 import jax.numpy as jnp
 from jax import lax
 from jax.sharding import PartitionSpec as P
+
+
+def in_order(blocks, dim):
+    blocks = jnp.moveaxis(blocks, 0, dim)
+    dims = blocks.shape
+    return blocks.reshape(*dims[:dim], dims[dim] * dims[dim + 1], *dims[dim + 2 :])
 
 
 def split_up(value, dim, length):
@@ -50,7 +56,19 @@
     target_col = own_block // col_blocks
     my_blocks = column_index * col_blocks + jnp.arange(col_blocks, dtype=jnp.int32)
     block_tiles = tiles_of(my_blocks)
-    widened = lax.all_gather(amplitudes, "row", axis=2, tiled=True)
+    peers = lax.axis_size("row")
+    pairs = [(i, (i + 1) % peers) for i in range(peers)]
+    back = [(b, a) for a, b in pairs]
+    lower, upper = ([], [])
+    for lap in range(peers - 1):
+        if lap % 2 == 0:
+            lower.append(lax.ppermute(lower[-1] if lower else amplitudes, "row", pairs))
+        else:
+            upper.append(lax.ppermute(upper[-1] if upper else amplitudes, "row", back))
+    blocks_2 = jnp.stack([*lower[::-1], amplitudes, *upper])
+    shift = lax.axis_index("row") - len(lower)
+    blocks_2 = blocks_2[(jnp.arange(peers) - shift) % peers]
+    widened = in_order(blocks_2, 2)
     widened = tile_recouple(widened, own_phases, own_orders)
     group_blocks = row_index * row_blocks + jnp.arange(row_blocks, dtype=jnp.int32)
     group_tiles = tiles_of(group_blocks)

time: 394 us -> 418 us (1.061)
  local copies, waits for them, and re-layouts: 53.2 us -> 76.9 us
  waiting for transfers between devices: 260 us -> 251 us
  starting transfers between devices: 9.24 us -> 18.2 us
    all_gather x1 -> x0, waiting for transfers between devices: 45.4 us -> none  [local(): widened = lax.all_gather(amplitudes, 'row', axis=2, tiled=True)]
    ppermute x0 -> x7, waiting for transfers between devices: none -> 37.7 us  [the longest x4 37.2 us: local(): lower.append(lax.ppermute(lower[-1] if lower else amplitudes, 'row', pairs))]
    unnamed x12 -> x19, local copies, waits for them, and re-layouts: 0.12 us -> 10.1 us
    ppermute x0 -> x7, starting transfers between devices: none -> 9.13 us  [the longest x3 9.12 us: local(): upper.append(lax.ppermute(upper[-1] if upper else amplitudes, 'row', back))]
    gather x0 -> x1, local copies, waits for them, and re-layouts: none -> 6.38 us  [local(): blocks_2 = blocks_2[(jnp.arange(peers) - shift) % peers]]
    reshape x0 -> x1, local copies, waits for them, and re-layouts: none -> 6.33 us  [in_order(): blocks.reshape(*dims[:dim], dims[dim] * dims[dim + 1], *dims[dim + 2:])]
  transfers between devices with their start and end apart: 4 -> 10, of which waited for: 4 -> 8; matrix products, arithmetic and copies ran while one was open for 2% -> 5% of each run, Pallas kernels for 0% -> 0%
where the time goes in v1:
time: 418 us; the launch traced here: 417 us
  waiting for transfers between devices  251 us (60%)
  local copies, waits for them, and re-layouts  76.9 us (18%)
  matrix products  31.7 us (8%)
  other arithmetic  23.6 us (6%)
  starting transfers between devices  18.2 us (4%)
  between operations  15.7 us (4%)
    psum x1, waiting for transfers between devices, local(): lax.psum(placed.reshape(row_blocks * tile_rows, widened.shape[2]), 'col')  142 us
    all_to_all x1, waiting for transfers between devices, sum_at_owner(): tiles = lax.all_to_all(split_up(value, dim, length), axis, 0, 0, tiled=True)  41.7 us
    gather x3, local copies, waits for them, and re-layouts, tile_recouple(): jnp.take(single, ordering, axis=0)  37.2 us
    ppermute x4, waiting for transfers between devices, local(): lower.append(lax.ppermute(lower[-1] if lower else amplitudes, 'row', pairs))  37.2 us
    dot_general x1, matrix products, local(): lax.dot_general(interaction, crossed, (((0,), (0,)), ((), ())), precision...  31.7 us
    all_to_all x1, waiting for transfers between devices, local(): lax.all_to_all(outgoing, 'col', split_axis=0, concat_axis=0, tiled=True)  29.7 us
    unnamed x19, local copies, waits for them, and re-layouts  10.1 us
    ppermute x3, starting transfers between devices, local(): upper.append(lax.ppermute(upper[-1] if upper else amplitudes, 'row', back))  9.12 us
  transfers between devices with their start and end apart: 10, of which 8 were waited for; matrix products, arithmetic and copies ran while one was open for 5% of the time, Pallas kernels for 0%

profile of v1, /device:TPU:0, one launch (start us, length us, event | category | flops | bytes accessed | tf_op | source)
XLA Modules:
  0.0 417.1 jit_solution(15846877001138141068)
XLA Ops:
  7.4 3.0 collective-permute-start.4
  10.3 9.9 %collective-permute-done = f32[6,256,128]{2,1,0:T(8,128)S(1)} collective-permute-done((f32[6,256,128]{2,1,0:T(8,128)}, f32[6,256,128]{2,1,0:T(8,128)S(1)}, u32[]{:S(2)}, u32[]{:S(2)}) %collective-permute-start) | collective-permute-done | bytes 786464 | tf_op jit(solution)/shard_map/ppermute | solution.py:65
  20.2 0.7 compare_and_fusion
  21.0 0.7 bitcast_or_fusion
  21.7 0.8 select_reduce_fusion.2
  22.5 0.7 subtract_convert_fusion
  23.2 9.6 %collective-permute-done.1 = f32[6,256,128]{2,1,0:T(8,128)S(1)} collective-permute-done((f32[6,256,128]{2,1,0:T(8,128)S(1)}, f32[6,256,128]{2,1,0:T(8,128)S(1)}, u32[]{:S(2)}, u32[]{:S(2)}) %collective-permute-start.1) | collective-permute-done | bytes 786464 | tf_op jit(solution)/shard_map/ppermute | solution.py:65
  32.9 0.8 select_reduce_fusion
  33.9 2.9 collective-permute-start.5
  36.8 8.7 %collective-permute-done.2 = f32[6,256,128]{2,1,0:T(8,128)} collective-permute-done((f32[6,256,128]{2,1,0:T(8,128)S(1)}, f32[6,256,128]{2,1,0:T(8,128)}, u32[]{:S(2)}, u32[]{:S(2)}) %collective-permute-start.2) | collective-permute-done | bytes 786464 | tf_op jit(solution)/shard_map/ppermute | solution.py:65
  45.8 0.5 collective-permute-done.5
  46.3 3.2 collective-permute-start.6
  49.6 9.0 %collective-permute-done.3 = f32[6,256,128]{2,1,0:T(8,128)} collective-permute-done((f32[6,256,128]{2,1,0:T(8,128)}, f32[6,256,128]{2,1,0:T(8,128)}, u32[]{:S(2)}, u32[]{:S(2)}) %collective-permute-start.3) | collective-permute-done | bytes 786464 | tf_op jit(solution)/shard_map/ppermute | solution.py:65
  58.5 2.1 bitcast_dynamic-update-slice_fusion.7
  60.6 2.1 bitcast_dynamic-update-slice_fusion.6
  62.7 1.0 bitcast_dynamic-update-slice_fusion.5
  63.6 0.9 bitcast_dynamic-update-slice_fusion.4
  64.6 0.9 bitcast_dynamic-update-slice_fusion.3
  65.5 0.9 bitcast_dynamic-update-slice_fusion.2
  66.4 2.1 bitcast_dynamic-update-slice_fusion.1
  68.5 1.0 bitcast_dynamic-update-slice_fusion
  69.5 6.4 %gather_fusion.1 = f32[8,6,256,128]{3,2,1,0:T(8,128)} fusion(f32[8,6,256,128]{3,2,1,0:T(8,128)} %bitcast_dynamic-update-slice_fusion, s32[1024]{0:T(1024)S(1)} %pad_clamp_fusion.3), kind=kCustom, calls=%fused_computation.1 | custom fusion | bytes 12582944 | tf_op jit(solution)/shard_map/gather | solution.py:70
  75.9 6.3 %copy_bitcast_fusion = f32[6,256,1024]{2,1,0:T(8,128)} fusion(f32[8,6,256,128]{3,2,1,0:T(8,128)} %gather_fusion.1), kind=kLoop, calls=%fused_computation.10 | loop fusion | bytes 12582912 | tf_op jit(solution)/shard_map/reshape | solution.py:10
  82.2 30.4 %gather_fusion.6 = f32[1536,1024]{1,0:T(8,128)} fusion(f32[6,256,1024]{2,1,0:T(8,128)} %copy_bitcast_fusion, s32[1536]{0:T(1024)S(1)} %reshape.282), kind=kCustom, calls=%fused_computation.6 | custom fusion | bytes 12595200 | tf_op jit(solution)/shard_map/vmap(jit(_take))/gather | solution.py:25
  112.6 4.8 %select_multiply_fusion = f32[6,256,1024]{2,1,0:T(8,128)} fusion(f32[6,256,1024]{2,1,0:T(8,128)} %bitcast.69, f32[6]{0:T(128)S(1)} %dynamic_slice.11, pred[6,256]{1,0:T(8,128)(4,1)S(1)} %compare_and_fusion), kind=kLoop, calls=%fused_computation.11 | loop fusion | flops 3145728 | bytes 12584472 | tf_op jit(solution)/shard_map/mul | solution.py:26
  117.4 7.1 %gather_fusion.2 = f32[8,256,1024]{2,1,0:T(8,128)} fusion(f32[6,256,1024]{2,1,0:T(8,128)} %select_multiply_fusion, s32[1024]{0:T(1024)S(1)} %get-tuple-element.25), kind=kCustom, calls=%fused_computation.2 | custom fusion | bytes 16777248 | tf_op jit(solution)/shard_map/jit(_take)/gather | solution.py:77
  124.5 5.8 %fusion = f32[2048,1024]{1,0:T(8,128)} fusion(f32[8,256,1024]{2,1,0:T(8,128)} %gather_fusion.2, f32[2048]{0:T(1024)S(1)} %bitcast.72, pred[2048]{0:T(1024)(128)(4,1)S(1)} %broadcast_in_dim.146), kind=kLoop, calls=%fused_computation.9 | loop fusion | flops 4194304 | bytes 16787456 | tf_op jit(solution)/shard_map/mul | solution.py:77
  130.3 142.0 %all-reduce.2.cloned.1.call-done = f32[2048,1024]{1,0:T(8,128)} async-done(((f32[2048,1024]{1,0:T(8,128)}), f32[2048,1024]{1,0:T(8,128)}) %all-reduce.2.cloned.1.call-update) | async-done | bytes 8388624 | tf_op jit(solution)/shard_map/psum | solution.py:79
  272.3 31.7 %fusion.7 = f32[1024,1024]{1,0:T(8,128)} fusion(f32[2048,1024]{1,0:T(8,128)} %all-reduce.2.cloned.1.call-done, f32[2048,1024]{1,0:T(8,128)} %param.8), kind=kOutput, calls=%fused_computation.78 | convolution fusion | flops 25769803776 | bytes 20971520 | tf_op jit(solution)/shard_map/dot_general | solution.py:80
  304.0 4.6 %all-to-all-start = ((f32[8,1024,128]{1,2,0:T(8,128)}), f32[8,1024,128]{1,2,0:T(8,128)}, u32[]{:S(2)}, u32[]{:S(2)}) async-start(f32[8,1024,128]{1,2,0:T(8,128)} %bitcast.70), calls=%async_computation | async-start | bytes 8388608 | tf_op jit(solution)/shard_map/all_to_all | solution.py:20
  308.5 0.2 sort.19.cloned.1.call-start
  308.8 0.6 gather_fusion.3
  309.4 1.5 gather_fusion
  310.9 0.7 broadcast_select_fusion
  311.6 0.6 iota.41
  312.3 2.8 sort.19.cloned.1.call-done
  315.1 0.7 fusion.1
  315.8 0.7 compare_and_fusion.1
  316.5 41.7 %all-to-all-done = f32[8,1024,128]{1,2,0:T(8,128)} async-done(((f32[8,1024,128]{1,2,0:T(8,128)}), f32[8,1024,128]{1,2,0:T(8,128)}, u32[]{:S(2)}, u32[]{:S(2)}) %all-to-all-start) | async-done | bytes 4194336 | tf_op jit(solution)/shard_map/all_to_all | solution.py:20
  358.2 2.6 reduce_sum.44
  361.0 6.8 %gather_fusion.7 = f32[1024,128]{1,0:T(8,128)S(1)} fusion(f32[4,256,128]{2,1,0:T(8,128)S(1)} %bitcast.68, s32[1024]{0:T(1024)S(1)} %bitcast.67), kind=kCustom, calls=%fused_computation.7 | custom fusion | bytes 1056768 | tf_op jit(solution)/shard_map/vmap(jit(_take))/gather | solution.py:25
  368.1 0.7 gather_fusion.4
  368.7 1.6 select_multiply_fusion.1
  370.4 4.5 %all-to-all-start.1 = ((f32[16,256,128]{2,1,0:T(8,128)}), f32[16,256,128]{2,1,0:T(8,128)S(1)}, u32[]{:S(2)}, u32[]{:S(2)}) async-start(f32[16,256,128]{2,1,0:T(8,128)} %select_multiply_fusion.1), calls=%async_computation.1 | async-start | bytes 4194304 | tf_op jit(solution)/shard_map/all_to_all | solution.py:98
  374.9 0.6 dynamic-slice.2
  376.3 29.7 %all-to-all-done.1 = f32[16,256,128]{2,1,0:T(8,128)S(1)} async-done(((f32[16,256,128]{2,1,0:T(8,128)}), f32[16,256,128]{2,1,0:T(8,128)S(1)}, u32[]{:S(2)}, u32[]{:S(2)}) %all-to-all-start.1) | async-done | bytes 2097184 | tf_op jit(solution)/shard_map/all_to_all | solution.py:98
  405.9 1.5 gather_fusion.5
  407.4 2.3 add_multiply_fusion
  (43 shorter events, 1.1 us)
Async XLA Ops:
  7.4 57.2 %copy-start = (f32[6,256,128]{2,1,0:T(8,128)S(1)}, f32[6,256,128]{2,1,0:T(8,128)}, u32[]{:S(2)}) copy-start(f32[6,256,128]{2,1,0:T(8,128)} %param.7) | copy-start | bytes 2359300
  7.4 265.0 %all-reduce.2.cloned.1.call-start = ((), (), s32[]{:S(2)}) async-start(), calls=%async_computation.2 | async-start | bytes 16777216 | tf_op jit(solution)/shard_map/psum | solution.py:79
  7.4 12.8 %collective-permute-start = (f32[6,256,128]{2,1,0:T(8,128)}, f32[6,256,128]{2,1,0:T(8,128)S(1)}, u32[]{:S(2)}, u32[]{:S(2)}) collective-permute-start(f32[6,256,128]{2,1,0:T(8,128)} %param.7), channel_id=1, source_target_pairs={{0,16},{16,32},{32,48},{48,64},{64,80},{80,96},{96,112},{112,0},{1... | collective-permute-start | bytes 2359304 | tf_op jit(solution)/shard_map/ppermute | solution.py:65
  7.4 26.5 %collective-permute-start.4 = (f32[6,256,128]{2,1,0:T(8,128)}, f32[6,256,128]{2,1,0:T(8,128)S(1)}, u32[]{:S(2)}, u32[]{:S(2)}) collective-permute-start(f32[6,256,128]{2,1,0:T(8,128)} %param.7), channel_id=1, source_target_pairs={{16,0},{32,16},{48,32},{64,48},{80,64},{96,80},{112,96},{0,112},{1... | collective-permute-start | bytes 2359304 | tf_op jit(solution)/shard_map/ppermute | solution.py:67
  20.2 12.6 %collective-permute-start.1 = (f32[6,256,128]{2,1,0:T(8,128)S(1)}, f32[6,256,128]{2,1,0:T(8,128)S(1)}, u32[]{:S(2)}, u32[]{:S(2)}) collective-permute-start(f32[6,256,128]{2,1,0:T(8,128)S(1)} %collective-permute-done), channel_id=1, source_target_pairs={{0,16},{16,32},{32,48},{48,64},{64,80},{80,96},{96,112},{112,0},{1... | collective-permute-start | bytes 2359304 | tf_op jit(solution)/shard_map/ppermute | solution.py:65
  32.8 12.7 %collective-permute-start.2 = (f32[6,256,128]{2,1,0:T(8,128)S(1)}, f32[6,256,128]{2,1,0:T(8,128)}, u32[]{:S(2)}, u32[]{:S(2)}) collective-permute-start(f32[6,256,128]{2,1,0:T(8,128)S(1)} %collective-permute-done.1), channel_id=1, source_target_pairs={{0,16},{16,32},{32,48},{48,64},{64,80},{80,96},{96,112},{112,0},{1... | collective-permute-start | bytes 2359304 | tf_op jit(solution)/shard_map/ppermute | solution.py:65
  33.9 12.5 %collective-permute-start.5 = (f32[6,256,128]{2,1,0:T(8,128)S(1)}, f32[6,256,128]{2,1,0:T(8,128)}, u32[]{:S(2)}, u32[]{:S(2)}) collective-permute-start(f32[6,256,128]{2,1,0:T(8,128)S(1)} %collective-permute-done.4), channel_id=1, source_target_pairs={{16,0},{32,16},{48,32},{64,48},{80,64},{96,80},{112,96},{0,112},{1... | collective-permute-start | bytes 2359304 | tf_op jit(solution)/shard_map/ppermute | solution.py:67
  45.6 12.9 %collective-permute-start.3 = (f32[6,256,128]{2,1,0:T(8,128)}, f32[6,256,128]{2,1,0:T(8,128)}, u32[]{:S(2)}, u32[]{:S(2)}) collective-permute-start(f32[6,256,128]{2,1,0:T(8,128)} %collective-permute-done.2), channel_id=1, source_target_pairs={{0,16},{16,32},{32,48},{48,64},{64,80},{80,96},{96,112},{112,0},{1... | collective-permute-start | bytes 2359304 | tf_op jit(solution)/shard_map/ppermute | solution.py:65
  46.3 22.2 %collective-permute-start.6 = (f32[6,256,128]{2,1,0:T(8,128)}, f32[6,256,128]{2,1,0:T(8,128)S(1)}, u32[]{:S(2)}, u32[]{:S(2)}) collective-permute-start(f32[6,256,128]{2,1,0:T(8,128)} %collective-permute-done.5), channel_id=1, source_target_pairs={{16,0},{32,16},{48,32},{64,48},{80,64},{96,80},{112,96},{0,112},{1... | collective-permute-start | bytes 2359304 | tf_op jit(solution)/shard_map/ppermute | solution.py:67
  304.0 54.2 %all-to-all-start = ((f32[8,1024,128]{1,2,0:T(8,128)}), f32[8,1024,128]{1,2,0:T(8,128)}, u32[]{:S(2)}, u32[]{:S(2)}) async-start(f32[8,1024,128]{1,2,0:T(8,128)} %bitcast.70), calls=%async_computation | async-start | bytes 8388608 | tf_op jit(solution)/shard_map/all_to_all | solution.py:20
  308.5 6.6 %sort.19.cloned.1.call-start = ((), (), s32[]{:S(2)}) async-start(), calls=%async_computation.3 | async-start | bytes 24608 | tf_op jit(solution)/shard_map/jit(argsort)/sort | solution.py:89
  368.0 6.9 %copy-start.3 = (s32[16]{0:T(128)S(1)}, s32[16]{0:T(128)}, u32[]{:S(2)}) copy-start(s32[16]{0:T(128)} %param.9) | copy-start | bytes 196
  368.0 8.1 %copy-start.2 = (s32[96]{0:T(128)S(1)}, s32[96]{0:T(128)}, u32[]{:S(2)}) copy-start(s32[96]{0:T(128)} %param.10) | copy-start | bytes 1156
  368.0 39.4 %copy-start.1 = (f32[6,256]{1,0:T(8,128)S(1)}, f32[6,256]{1,0:T(8,128)}, u32[]{:S(2)}) copy-start(f32[6,256]{1,0:T(8,128)} %param.13) | copy-start | bytes 18436
  370.4 35.5 %all-to-all-start.1 = ((f32[16,256,128]{2,1,0:T(8,128)}), f32[16,256,128]{2,1,0:T(8,128)S(1)}, u32[]{:S(2)}, u32[]{:S(2)}) async-start(f32[16,256,128]{2,1,0:T(8,128)} %select_multiply_fusion.1), calls=%async_computation.1 | async-start | bytes 4194304 | tf_op jit(solution)/shard_map/all_to_all | solution.py:98
Sparse Core Ops, SparseCore 0:
  130.5 141.8 all-reduce.1
Sparse Core Ops, SparseCore 1:
  312.3 2.5 sort.21.cloned.1.call-done
  (1 shorter events, 0.0 us)
